TPU v7x, 256 devices: a whole 4x4x8 slice. The times are simulated.
256 devices in a mesh: tm: 8 (over z), seq: 32 (over y, x, core).
Axes of the slice: x: 4, y: 4, z: 8, core: 2. Of those that a mesh axis runs over, the one named last changes fastest.
Arguments:
- states: float32 [64, 1536, 64], P('tm', 'seq'), may hold values from -11 to 11
- first_state: float32 [1536, 64], P('seq'), may hold values from -6 to 6
- now_step: int32 [64], P('tm'), may hold values from 1 to 960, as said below
- next_step: int32 [64], P('tm'), may hold values from 0 to 959, as said below
- embed_weight: bfloat16 [64, 1536], replicated, may hold values from -0.75 to 0.75
- mod_weight: bfloat16 [256, 4608], replicated, may hold values from -0.375 to 0.375
- qkv_weight: bfloat16 [1536, 12, 384], P('seq'), may hold values from -1 to 1
- out_weight: bfloat16 [1536, 1536], P('seq'), may hold values from -0.15625 to 0.15625
- final_weight: bfloat16 [1536, 64], replicated, may hold values from -0.15625 to 0.15625
Outputs:
- advanced: float32 [64, 1536, 64], P('tm', 'seq')
- errors: float32 [64], P('tm')
Inputs may be any that keep to these rules, and one draw needn't show every extreme that they name: now_step[0] = 960 and now_step[j + 1] = next_step[j]. next_step[j] is now_step[j] minus a gap of 1 to 15.
All inputs are finite; a program needn't handle non-finite values.
Results may differ from a plain program's by a relative error of at most 0.002.
Values may be sent and summed in bfloat16 or wider, within the bound.
A program may use at most 64 MiB of HBM per device.

v0:
```python
import math
import jax
import jax.numpy as jnp
from jax import lax
from jax.sharding import PartitionSpec as P


def from_behind(shard, axis, by):
    count = lax.axis_size(axis)
    pairs = [(i, i + by) for i in range(count) if 0 <= i + by < count]
    return lax.ppermute(shard, axis, pairs)


def entering(part, axis, combine, identity):
    place = lax.axis_index(axis)
    gathered = lax.all_gather(part, axis)
    state = jnp.zeros_like(part) + jnp.asarray(identity, part.dtype)

    def one(step, state):
        return combine(state, lax.dynamic_index_in_dim(gathered, step, 0, False))

    return lax.fori_loop(0, place, one, state)


def layer_norm(rows):
    row_mean = jnp.mean(rows, axis=-1, keepdims=True)
    centered = rows - row_mean
    variance = jnp.mean(centered * centered, axis=-1, keepdims=True)
    return centered * lax.rsqrt(variance + 1e-06)


def alpha_bar(step_ids):
    fraction = (step_ids.astype(jnp.float32) / 1000.0 + 0.008) / 1.008
    return jnp.cos(fraction * (math.pi / 2)) ** 2


def coefficients(now_step, next_step):
    alpha_now = alpha_bar(now_step)
    alpha_next = alpha_bar(next_step)
    step_ratio = jnp.sqrt(alpha_next / alpha_now)
    keep_coef = step_ratio - 1.0
    noise_coef = jnp.sqrt(1.0 - alpha_next) - step_ratio * jnp.sqrt(1.0 - alpha_now)
    return (keep_coef, noise_coef)


def modulation(step_ids, mod_weight):
    half_freq = mod_weight.shape[0] // 2
    frequency = jnp.exp(-math.log(10000.0) * jnp.arange(half_freq, dtype=jnp.float32) / half_freq)
    angles = step_ids.astype(jnp.float32)[:, None] * frequency[None, :]
    time_embed = jnp.concatenate([jnp.cos(angles), jnp.sin(angles)], axis=1).astype(jnp.bfloat16)
    return jnp.dot(time_embed, mod_weight, preferred_element_type=jnp.float32)


def attend_one(pair_item):
    hdim = pair_item.shape[1] // 3
    length = pair_item.shape[0]
    query_rows = 512
    queries = pair_item[:, :hdim]
    key_rows = pair_item[:, hdim : 2 * hdim]
    values = pair_item[:, 2 * hdim :]

    def one_block(query_block):
        scores = jnp.dot(query_block, key_rows.T, preferred_element_type=jnp.float32) * hdim ** (
            -0.5
        )
        row_max = jnp.max(scores, axis=1, keepdims=True)
        exponent = jnp.exp(scores - row_max)
        weights = (exponent / jnp.sum(exponent, axis=1, keepdims=True)).astype(jnp.bfloat16)
        return jnp.dot(weights, values, preferred_element_type=jnp.float32).astype(jnp.bfloat16)

    blocks_out = lax.map(one_block, queries.reshape(length // query_rows, query_rows, hdim))
    return blocks_out.reshape(length, hdim)


def attend_pairs(pair_block):
    return lax.map(attend_one, pair_block[0])[None]


def add_terms(earlier, later):
    return earlier + later


def per_device(
    states,
    first_state,
    now_step,
    next_step,
    embed_weight,
    mod_weight,
    qkv_weight,
    out_weight,
    final_weight,
):
    step_count, tokd, chans = states.shape
    seq_devs = lax.axis_size("seq")
    time_index = lax.axis_index("tm")
    heads = qkv_weight.shape[1]
    width_three = qkv_weight.shape[2]
    hdim = width_three // 3
    width = heads * hdim
    edge_state = from_behind(states[-1], "tm", 1)
    opening = jnp.where(time_index == 0, first_state, edge_state)
    previous = jnp.concatenate([opening[None], states[:-1]], axis=0)
    keep_coef, noise_coef = coefficients(now_step, next_step)
    modulated_all = modulation(now_step, mod_weight)
    shift_mod = modulated_all[:, :width]
    scale_mod = modulated_all[:, width : 2 * width]
    gate_mod = modulated_all[:, 2 * width :]
    residual = jnp.einsum(
        "tsc,cd->tsd",
        previous.astype(jnp.bfloat16),
        embed_weight,
        preferred_element_type=jnp.float32,
    )
    modulated = (
        layer_norm(residual) * (1.0 + scale_mod[:, None, :]) + shift_mod[:, None, :]
    ).astype(jnp.bfloat16)
    columns = modulated
    projected = jnp.einsum(
        "tsd,dhc->thsc",
        columns,
        lax.all_gather(qkv_weight, "seq", axis=0, tiled=True),
        preferred_element_type=jnp.float32,
    ).astype(jnp.bfloat16)
    pair_count = step_count * heads
    per_dev = pair_count // seq_devs
    grouped = projected.reshape(seq_devs, per_dev, tokd, width_three)
    routed = attend_pairs(lax.all_to_all(grouped, "seq", split_axis=0, concat_axis=2, tiled=True))
    returned = lax.all_to_all(routed, "seq", split_axis=2, concat_axis=0, tiled=True)
    flattened = jnp.transpose(
        returned.reshape(step_count, heads, tokd, hdim), (0, 2, 1, 3)
    ).reshape(step_count, tokd, width)
    columns = flattened
    projection = jnp.einsum(
        "tsd,de->tse",
        columns,
        lax.all_gather(out_weight, "seq", axis=0, tiled=True),
        preferred_element_type=jnp.float32,
    )
    updated = residual + gate_mod[:, None, :] * projection
    normed_out = layer_norm(updated).astype(jnp.bfloat16)
    noise_pred = jnp.einsum(
        "tsd,dc->tsc", normed_out, final_weight, preferred_element_type=jnp.float32
    )
    drift_terms = keep_coef[:, None, None] * previous + noise_coef[:, None, None] * noise_pred
    running_sums = jnp.cumsum(drift_terms, axis=0)
    block_total = running_sums[-1]
    carried = entering(block_total, "tm", add_terms, jnp.zeros_like(block_total))
    advanced = first_state[None] + carried[None] + running_sums
    difference = advanced - states
    partial_value = jnp.sum(difference * difference, axis=(1, 2))
    errors = lax.psum(partial_value, "seq") / (tokd * seq_devs * chans)
    return (advanced, errors)


def solution(mesh):
    in_specs = (
        P("tm", "seq", None),
        P("seq", None),
        P("tm"),
        P("tm"),
        P(),
        P(),
        P("seq", None, None),
        P("seq", None),
        P(),
    )
    out_specs = (P("tm", "seq", None), P("tm"))
    return jax.shard_map(
        per_device, mesh=mesh, in_specs=in_specs, out_specs=out_specs, check_vma=False
    )
```

profile of v0, /device:TPU:1, one launch (start us, length us, event | category | flops | bytes accessed | tf_op | source)
XLA Modules:
  0.0 330.8 jit_solution(13507943861712329472)
XLA Ops:
  7.3 0.7 all-gather.3.cloned.1.call-update
  7.9 0.8 slice_bitcast_fusion
  8.8 4.3 %collective-permute-start = (f32[48,64]{1,0:T(8,128)S(1)}, f32[48,64]{1,0:T(8,128)S(1)}, u32[]{:S(2)}, u32[]{:S(2)}) collective-permute-start(f32[48,64]{1,0:T(8,128)S(1)} %slice_bitcast_fusion), channel_id=1, source_target_pairs={{0,32},{32,64},{64,96},{96,128},{128,160},{160,192},{192,224},{1,3... | collective-permute-start | bytes 36872 | tf_op jit(solution)/shard_map/ppermute | solution.py:11
  13.1 0.7 convert_element_type.30
  14.3 0.6 fusion.53
  16.2 1.4 copy-done.1
  18.0 68.3 %all-gather.3.cloned.1.call-done = bf16[1536,12,384]{2,0,1:T(8,128)(2,1)} async-done(((bf16[48,12,384]{2,0,1:T(8,128)(2,1)}), bf16[1536,12,384]{2,0,1:T(8,128)(2,1)}) %all-gather.3.cloned.1.call-update) | async-done | bytes 14155792 | tf_op jit(solution)/shard_map/all_gather | solution.py:122
  86.3 11.1 %fusion.18 = bf16[8,48,12,384]{3,1,2,0:T(8,128)(2,1)} fusion(bf16[1536,12,384]{2,0,1:T(8,128)(2,1)} %all-gather.3.cloned.1.call-done, f32[8,48,1536]{2,1,0:T(8,128)} %copy-done.1, f32[8,1536]{1,0:T(8,128)S(1)} %get-tuple-element.105, f32[8,1536]{1,0:T(8,128)S(1)} %get-tuple-element.106, f32[8,48]{1,0:T(8,128)S(1)} %add_rsqrt_fusion.1, ...), kind=kOutput, calls=%fused_computation.20 | convolution fusion | flops 5440536576 | bytes 20155392 | tf_op jit(solution)/shard_map/tsd,dhc->thsc/dot_general | solution.py:119
  97.3 5.5 %all-to-all-start = ((bf16[32,3,48,384]{3,2,1,0:T(8,128)(2,1)}), bf16[32,3,48,384]{3,2,1,0:T(8,128)(2,1)}, u32[]{:S(2)}, u32[]{:S(2)}) async-start(bf16[32,3,48,384]{3,2,1,0:T(8,128)(2,1)} %bitcast.93), calls=%async_computation | async-start | bytes 7077888 | tf_op jit(solution)/shard_map/all_to_all | solution.py:128
  102.8 0.7 all-gather.5.cloned.1.call-update
  103.6 44.9 %all-to-all-done = bf16[32,3,48,384]{3,2,1,0:T(8,128)(2,1)} async-done(((bf16[32,3,48,384]{3,2,1,0:T(8,128)(2,1)}), bf16[32,3,48,384]{3,2,1,0:T(8,128)(2,1)}, u32[]{:S(2)}, u32[]{:S(2)}) %all-to-all-start) | async-done | bytes 3538976 | tf_op jit(solution)/shard_map/all_to_all | solution.py:128
  148.5 4.1 %copy.17 = bf16[1,3,32,48,384]{4,3,2,1,0:T(8,128)(2,1)} copy(bf16[1,3,32,48,384]{4,3,1,2,0:T(8,128)(2,1)} %bitcast.15) | data formatting | bytes 7077888 | tf_op jit(solution)/shard_map/all_to_all | solution.py:128
  152.6 33.7 %while.31 = (s32[]{:T(128)}, bf16[3,1536,128]{2,1,0:T(8,128)(2,1)}, bf16[3,1536,384]{2,1,0:T(8,128)(2,1)}, s32[]{:T(128)}, s32[]{:T(128)}, /*index=5*/s32[]{:T(128)}) while((s32[]{:T(128)}, bf16[3,1536,128]{2,1,0:T(8,128)(2,1)}, bf16[3,1536,384]{2,1,0:T(8,128)(2,1)}, s32[]{:T(128)}, s32[]{:T(128)}, /*index=5*/s32[]{:T(128)}) %tuple.79), condition=%wide.region_7.8_spmd, body=%wide.region_2.7_spmd.sunk | while | flops 408222720 | bytes 16002250 | solution.py:76
  152.6 1.4 dynamic-slice_bitcast_fusion.2
  154.2 7.8 %while.33 = (s32[]{:T(128)}, bf16[3,512,128]{2,1,0:T(8,128)(2,1)}, bf16[3,512,128]{2,1,0:T(8,128)(2,1)S(1)}, bf16[1536,128]{1,0:T(8,128)(2,1)S(1)}, bf16[1536,128]{1,0:T(8,128)(2,1)S(1)}, /*index=5*/s32[]{:T(128)}) while((s32[]{:T(128)}, bf16[3,512,128]{2,1,0:T(8,128)(2,1)}, bf16[3,512,128]{2,1,0:T(8,128)(2,1)S(1)}, ...), condition=%wide.region_6.6_spmd, body=%wide.region_3.5_spmd.sunk | while | flops 408222720 | bytes 10496585 | solution.py:71
  154.2 0.7 fusion.68
  155.5 1.4 fusion.70
  156.8 0.7 fusion.68
  158.1 1.4 fusion.70
  159.5 0.7 fusion.68
  160.7 1.4 fusion.70
  162.1 1.8 bitcast_dynamic-update-slice_fusion.2
  163.8 1.4 dynamic-slice_bitcast_fusion.2
  165.5 7.8 %while.33 = (s32[]{:T(128)}, bf16[3,512,128]{2,1,0:T(8,128)(2,1)}, bf16[3,512,128]{2,1,0:T(8,128)(2,1)S(1)}, bf16[1536,128]{1,0:T(8,128)(2,1)S(1)}, bf16[1536,128]{1,0:T(8,128)(2,1)S(1)}, /*index=5*/s32[]{:T(128)}) while((s32[]{:T(128)}, bf16[3,512,128]{2,1,0:T(8,128)(2,1)}, bf16[3,512,128]{2,1,0:T(8,128)(2,1)S(1)}, ...), condition=%wide.region_6.6_spmd, body=%wide.region_3.5_spmd.sunk | while | flops 408222720 | bytes 10496585 | solution.py:71
  165.5 0.7 fusion.68
  166.7 1.4 fusion.70
  168.1 0.7 fusion.68
  169.3 1.4 fusion.70
  170.7 0.7 fusion.68
  171.9 1.4 fusion.70
  173.3 1.8 bitcast_dynamic-update-slice_fusion.2
  175.1 1.4 dynamic-slice_bitcast_fusion.2
  176.7 7.8 %while.33 = (s32[]{:T(128)}, bf16[3,512,128]{2,1,0:T(8,128)(2,1)}, bf16[3,512,128]{2,1,0:T(8,128)(2,1)S(1)}, bf16[1536,128]{1,0:T(8,128)(2,1)S(1)}, bf16[1536,128]{1,0:T(8,128)(2,1)S(1)}, /*index=5*/s32[]{:T(128)}) while((s32[]{:T(128)}, bf16[3,512,128]{2,1,0:T(8,128)(2,1)}, bf16[3,512,128]{2,1,0:T(8,128)(2,1)S(1)}, ...), condition=%wide.region_6.6_spmd, body=%wide.region_3.5_spmd.sunk | while | flops 408222720 | bytes 10496585 | solution.py:71
  176.7 0.7 fusion.68
  177.9 1.4 fusion.70
  179.3 0.7 fusion.68
  180.6 1.4 fusion.70
  181.9 0.7 fusion.68
  183.2 1.4 fusion.70
  184.6 1.8 bitcast_dynamic-update-slice_fusion.2
  186.3 8.1 %copy.31 = bf16[3,1536,128]{2,0,1:T(4,128)(2,1)} copy(bf16[3,1536,128]{2,1,0:T(8,128)(2,1)} %get-tuple-element.69) | data formatting | bytes 2359296 | tf_op jit(solution)/shard_map/while | solution.py:76
  194.4 7.4 %all-to-all-start.1 = ((bf16[1,3,1536,128]{3,1,0,2:T(4,128)(2,1)}), bf16[1,3,1536,128]{3,1,0,2:T(4,128)(2,1)}, u32[]{:S(2)}, u32[]{:S(2)}) async-start(bf16[1,3,1536,128]{3,1,0,2:T(4,128)(2,1)} %bitcast.91), calls=%async_computation.1 | async-start | bytes 3145728 | tf_op jit(solution)/shard_map/all_to_all | solution.py:129
  202.0 22.2 %all-to-all-done.1 = bf16[1,3,1536,128]{3,1,0,2:T(4,128)(2,1)} async-done(((bf16[1,3,1536,128]{3,1,0,2:T(4,128)(2,1)}), bf16[1,3,1536,128]{3,1,0,2:T(4,128)(2,1)}, u32[]{:S(2)}, u32[]{:S(2)}) %all-to-all-start.1) | async-done | bytes 1179680 | tf_op jit(solution)/shard_map/all_to_all | solution.py:129
  224.2 1.6 copy.19
  225.9 5.1 %fusion.55 = (f32[8,48]{1,0:T(8,128)S(1)}, f32[8,48,1536]{2,1,0:T(8,128)S(1)}) fusion(f32[8,48,1536]{2,1,0:T(8,128)} %copy-done.1, bf16[1536,1536]{1,0:T(8,128)(2,1)} %all-gather.5.cloned.1.call-done, bf16[8,12,6,8,128]{4,3,2,1,0:T(8,128)(2,1)S(1)} %bitcast.94, f32[8,1536]{1,0:T(8,128)} %get-tuple-element.104), kind=kOutput, calls=%fused_computation.77 | convolution fusion | flops 1813708416 | bytes 10667520 | tf_op jit(solution)/shard_map/tsd,de->tse/dot_general | solution.py:134
  232.6 20.1 %all_gather.11 = f32[8,48,64]{2,1,0:T(8,128)S(1)} all-gather(f32[1,48,64]{2,1,0:T(8,128)S(1)} %slice.39), channel_id=1, replica_groups=mesh['tm'=8,'seq'=32] {'tm'}, dimensions={0}, use_global_device_ids=true | all-gather | bytes 110592 | tf_op jit(solution)/shard_map/all_gather | solution.py:16
  252.8 0.7 multiply_reduce_fusion.2
  253.5 70.0 %psum.7 = f32[8]{0:T(128)S(1)} all-reduce(f32[8]{0:T(128)S(1)} %get-tuple-element.95), channel_id=1, replica_groups=mesh['tm'=8,'seq'=32] {'seq'}, use_global_device_ids=true, to_apply=%region_14.15 | all-reduce | flops 8 | bytes 64 | tf_op jit(solution)/shard_map/psum | solution.py:152
  (69 shorter events, 10.2 us)
Async XLA Ops:
  7.2 6.7 %copy-start = (bf16[256,4608]{1,0:T(8,128)(2,1)S(1)}, bf16[256,4608]{1,0:T(8,128)(2,1)}, u32[]{:S(2)}) copy-start(bf16[256,4608]{1,0:T(8,128)(2,1)} %param.20) | copy-start | bytes 7077892
  7.2 7.8 %copy-start.4 = (f32[8,48,64]{2,1,0:T(8,128)S(1)}, f32[8,48,64]{2,1,0:T(8,128)}, u32[]{:S(2)}) copy-start(f32[8,48,64]{2,1,0:T(8,128)} %param.15) | copy-start | bytes 294916
  7.2 7.8 %copy-start.10 = (f32[48,64]{1,0:T(8,128)S(1)}, f32[48,64]{1,0:T(8,128)}, u32[]{:S(2)}) copy-start(f32[48,64]{1,0:T(8,128)} %param.16) | copy-start | bytes 36868
  7.2 8.4 %copy-start.9 = (bf16[64,1536]{1,0:T(8,128)(2,1)S(1)}, bf16[64,1536]{1,0:T(8,128)(2,1)}, u32[]{:S(2)}) copy-start(bf16[64,1536]{1,0:T(8,128)(2,1)} %param.19) | copy-start | bytes 589828
  7.2 79.0 %all-gather.3.cloned.1.call-start = ((), (), s32[]{:S(2)}) async-start(), calls=%async_computation.2 | async-start | bytes 14598144 | tf_op jit(solution)/shard_map/all_gather | solution.py:122
  8.8 6.2 %collective-permute-start = (f32[48,64]{1,0:T(8,128)S(1)}, f32[48,64]{1,0:T(8,128)S(1)}, u32[]{:S(2)}, u32[]{:S(2)}) collective-permute-start(f32[48,64]{1,0:T(8,128)S(1)} %slice_bitcast_fusion), channel_id=1, source_target_pairs={{0,32},{32,64},{64,96},{96,128},{128,160},{160,192},{192,224},{1,3... | collective-permute-start | bytes 36872 | tf_op jit(solution)/shard_map/ppermute | solution.py:11
  15.0 3.0 copy-start.2
  15.0 0.6 copy-start.6
  16.2 1.4 copy-start.1
  97.3 51.2 %all-to-all-start = ((bf16[32,3,48,384]{3,2,1,0:T(8,128)(2,1)}), bf16[32,3,48,384]{3,2,1,0:T(8,128)(2,1)}, u32[]{:S(2)}, u32[]{:S(2)}) async-start(bf16[32,3,48,384]{3,2,1,0:T(8,128)(2,1)} %bitcast.93), calls=%async_computation | async-start | bytes 7077888 | tf_op jit(solution)/shard_map/all_to_all | solution.py:128
  102.8 123.1 %all-gather.5.cloned.1.call-start = ((), (), s32[]{:S(2)}) async-start(), calls=%async_computation.3 | async-start | bytes 4866048 | tf_op jit(solution)/shard_map/all_gather | solution.py:137
  186.3 15.5 %copy-start.12 = (s32[8]{0:T(128)S(1)}, s32[8]{0:T(128)}, u32[]{:S(2)}) copy-start(s32[8]{0:T(128)} %param.17) | copy-start | bytes 100
  186.3 15.5 %copy-start.13 = (s32[8]{0:T(128)S(1)}, s32[8]{0:T(128)}, u32[]{:S(2)}) copy-start(s32[8]{0:T(128)} %param.18) | copy-start | bytes 100
  194.4 29.8 %all-to-all-start.1 = ((bf16[1,3,1536,128]{3,1,0,2:T(4,128)(2,1)}), bf16[1,3,1536,128]{3,1,0,2:T(4,128)(2,1)}, u32[]{:S(2)}, u32[]{:S(2)}) async-start(bf16[1,3,1536,128]{3,1,0,2:T(4,128)(2,1)} %bitcast.91), calls=%async_computation.1 | async-start | bytes 3145728 | tf_op jit(solution)/shard_map/all_to_all | solution.py:129
  231.0 0.9 copy-start.8
  231.1 1.5 copy-start.3
  231.1 1.4 copy-start.7
  231.5 21.3 %copy-start.11 = (f32[48,64]{1,0:T(8,128)S(1)}, f32[48,64]{1,0:T(8,128)}, u32[]{:S(2)}) copy-start(f32[48,64]{1,0:T(8,128)} %param.16) | copy-start | bytes 36868
  231.5 21.3 %copy-start.5 = (f32[8,48,64]{2,1,0:T(8,128)S(1)}, f32[8,48,64]{2,1,0:T(8,128)}, u32[]{:S(2)}) copy-start(f32[8,48,64]{2,1,0:T(8,128)} %param.15) | copy-start | bytes 294916
Sparse Core Ops, SparseCore 0:
  10.7 75.5 all-gather.2
  106.2 68.7 all-gather.4
where the time goes:
time: 331 us
  waiting for transfers between devices  137 us (41%)
  blocking collectives  90.1 us (27%)
  matrix products  36 us (11%)
  local copies, waits for them, and re-layouts  27.4 us (8%)
  starting transfers between devices  17.3 us (5%)
  between operations  14.4 us (4%)
  other arithmetic  8.79 us (3%)
    psum x1, blocking collectives, per_device(): errors = lax.psum(partial_value, 'seq') / (tokd * seq_devs * chans)  70 us
    all_gather x1, waiting for transfers between devices, per_device(): lax.all_gather(qkv_weight, 'seq', axis=0, tiled=True)  68.3 us
    all_to_all x1, waiting for transfers between devices, per_device(): lax.all_to_all(grouped, 'seq', split_axis=0, concat_axis=2, tiled=True)  44.9 us
    all_to_all x1, waiting for transfers between devices, per_device(): lax.all_to_all(routed, 'seq', split_axis=2, concat_axis=0, tiled=True)  22.2 us
    all_gather x1, blocking collectives, entering(): gathered = lax.all_gather(part, axis)  20.1 us
    dot_general x9, matrix products, one_block(): jnp.dot(weights, values, preferred_element_type=jnp.float32)  12.4 us
    dot_general x1, matrix products, per_device(): jnp.einsum('tsd,dhc->thsc', columns, lax.all_gather(qkv_weight, 'seq', ax...  11.1 us
    while x1, local copies, waits for them, and re-layouts, attend_pairs(): return lax.map(attend_one, pair_block[0])[None]  8.06 us
  transfers between devices with their start and end apart: 5, of which 3 were waited for; matrix products, arithmetic and copies ran while one was open for 15% of the time, Pallas kernels for 0%

commit v1 on v0

--- a/solution.py
+++ b/solution.py
@@ -119,7 +119,9 @@
     projected = jnp.einsum(
         "tsd,dhc->thsc",
         columns,
-        lax.all_gather(qkv_weight, "seq", axis=0, tiled=True),
+        jnp.concatenate(
+            lax.all_to_all(jnp.stack([qkv_weight] * lax.axis_size("seq")), "seq", 0, 0), axis=0
+        ),
         preferred_element_type=jnp.float32,
     ).astype(jnp.bfloat16)
     pair_count = step_count * heads

time: 331 us -> 444 us (1.34)
  waiting for transfers between devices: 137 us -> 232 us
  starting transfers between devices: 17.3 us -> 33.9 us
  matrix products: 36 us -> 26.3 us
  local copies, waits for them, and re-layouts: 27.4 us -> 35.3 us
    all_to_all x0 -> x1, waiting for transfers between devices: none -> 164 us  [per_device(): lax.all_to_all(jnp.stack([qkv_weight] * lax.axis_size('seq')), 'seq', 0, 0)]
    all_gather x1 -> x0, waiting for transfers between devices: 68.3 us -> none  [per_device(): lax.all_gather(qkv_weight, 'seq', axis=0, tiled=True)]
    all_to_all x1, starting transfers between devices: 5.48 us -> 14.2 us  [per_device(): lax.all_to_all(grouped, 'seq', split_axis=0, concat_axis=2, tiled=True)]
    all_to_all x0 -> x1, starting transfers between devices: none -> 8.76 us  [per_device(): lax.all_to_all(jnp.stack([qkv_weight] * lax.axis_size('seq')), 'seq', 0, 0)]
    another operation x0 -> x1, local copies, waits for them, and re-layouts: none -> 8.4 us  [per_device(): jnp.stack([qkv_weight] * lax.axis_size('seq'))]
    all_to_all x0 -> x1, local copies, waits for them, and re-layouts: none -> 6.77 us  [per_device(): lax.all_to_all(jnp.stack([qkv_weight] * lax.axis_size('seq')), 'seq', 0, 0)]
    dot_general x9, matrix products: 12.4 us -> 6.97 us  [one_block(): jnp.dot(weights, values, preferred_element_type=jnp.float32)]
    dynamic_update_slice x3, local copies, waits for them, and re-layouts: 5.33 us -> 0.17 us  [attend_pairs(): return lax.map(attend_one, pair_block[0])[None]]
  transfers between devices with their start and end apart: 5 -> 5, of which waited for: 3 -> 3; matrix products, arithmetic and copies ran while one was open for 15% -> 9% of each run, Pallas kernels for 0% -> 0%
where the time goes in v1:
time: 444 us; the launch traced here: 443 us
  waiting for transfers between devices  232 us (52%)
  blocking collectives  93 us (21%)
  local copies, waits for them, and re-layouts  35.3 us (8%)
  starting transfers between devices  33.9 us (8%)
  matrix products  26.3 us (6%)
  between operations  14.5 us (3%)
  other arithmetic  8.14 us (2%)
    all_to_all x1, waiting for transfers between devices, per_device(): lax.all_to_all(jnp.stack([qkv_weight] * lax.axis_size('seq')), 'seq', 0, 0)  164 us
    psum x1, blocking collectives, per_device(): errors = lax.psum(partial_value, 'seq') / (tokd * seq_devs * chans)  70.3 us
    all_to_all x1, waiting for transfers between devices, per_device(): lax.all_to_all(grouped, 'seq', split_axis=0, concat_axis=2, tiled=True)  44.9 us
    all_gather x1, blocking collectives, entering(): gathered = lax.all_gather(part, axis)  22.7 us
    all_to_all x1, waiting for transfers between devices, per_device(): lax.all_to_all(routed, 'seq', split_axis=2, concat_axis=0, tiled=True)  22.2 us
    all_to_all x1, starting transfers between devices, per_device(): lax.all_to_all(grouped, 'seq', split_axis=0, concat_axis=2, tiled=True)  14.2 us
  transfers between devices with their start and end apart: 5, of which 3 were waited for; matrix products, arithmetic and copies ran while one was open for 9% of the time, Pallas kernels for 0%

profile of v1, /device:TPU:1, one launch (start us, length us, event | category | flops | bytes accessed | tf_op | source)
XLA Modules:
  0.0 443.2 jit_solution(602182317919827615)
XLA Ops:
  7.2 8.4 %stack.2 = bf16[32,48,12,384]{3,1,2,0:T(8,128)(2,1)} broadcast(bf16[48,12,384]{2,0,1:T(8,128)(2,1)} %param.21), dimensions={1,2,3} | broadcast | bytes 14598144 | tf_op jit(solution)/shard_map/stack | solution.py:123
  15.6 8.8 %all-to-all-start = ((bf16[32,48,12,384]{3,1,2,0:T(8,128)(2,1)}), bf16[32,48,12,384]{3,1,2,0:T(8,128)(2,1)}, u32[]{:S(2)}, u32[]{:S(2)}) async-start(bf16[32,48,12,384]{3,1,2,0:T(8,128)(2,1)} %stack.2), calls=%async_computation | async-start | bytes 28311552 | tf_op jit(solution)/shard_map/all_to_all | solution.py:123
  24.4 3.7 collective-permute-start
  28.6 0.6 fusion.48
  29.4 0.6 copy-done.8
  30.9 164.2 %all-to-all-done = bf16[32,48,12,384]{3,1,2,0:T(8,128)(2,1)} async-done(((bf16[32,48,12,384]{3,1,2,0:T(8,128)(2,1)}), bf16[32,48,12,384]{3,1,2,0:T(8,128)(2,1)}, u32[]{:S(2)}, u32[]{:S(2)}) %all-to-all-start) | async-done | bytes 14155808 | tf_op jit(solution)/shard_map/all_to_all | solution.py:123
  195.1 6.8 %copy.17 = bf16[32,48,12,384]{3,1,0,2:T(8,128)(2,1)S(1)} copy(bf16[32,48,12,384]{3,1,2,0:T(8,128)(2,1)} %all-to-all-done) | data formatting | bytes 28311552 | tf_op jit(solution)/shard_map/all_to_all | solution.py:123
  201.9 7.6 %convolution_convert_fusion = bf16[8,48,12,384]{3,1,2,0:T(8,128)(2,1)} fusion(bf16[1536,12,384,1]{2,0,1,3:T(8,128)(2,1)S(1)} %bitcast.90, f32[8,48,1536]{2,1,0:T(8,128)S(1)} %get-tuple-element.110, f32[8,1536]{1,0:T(8,128)S(1)} %get-tuple-element.105, f32[8,1536]{1,0:T(8,128)S(1)} %get-tuple-element.106, f32[8,48]{1,0:T(8,128)S(1)} %add_rsqrt_fusion.1, ...), kind=kOutput, calls=%fused_computation.18 | convolution fusion | flops 5440536576 | bytes 20155392 | tf_op jit(solution)/shard_map/tsd,dhc->thsc/dot_general | solution.py:119
  209.4 14.2 %all-to-all-start.1 = ((bf16[32,3,48,384]{3,2,1,0:T(8,128)(2,1)}), bf16[32,3,48,384]{3,2,1,0:T(8,128)(2,1)}, u32[]{:S(2)}, u32[]{:S(2)}) async-start(bf16[32,3,48,384]{3,2,1,0:T(8,128)(2,1)} %bitcast.93), calls=%async_computation.1 | async-start | bytes 7077888 | tf_op jit(solution)/shard_map/all_to_all | solution.py:130
  224.4 44.9 %all-to-all-done.1 = bf16[32,3,48,384]{3,2,1,0:T(8,128)(2,1)} async-done(((bf16[32,3,48,384]{3,2,1,0:T(8,128)(2,1)}), bf16[32,3,48,384]{3,2,1,0:T(8,128)(2,1)}, u32[]{:S(2)}, u32[]{:S(2)}) %all-to-all-start.1) | async-done | bytes 3538976 | tf_op jit(solution)/shard_map/all_to_all | solution.py:130
  269.3 4.1 copy.18
  273.4 23.3 %while.31 = (s32[]{:T(128)}, bf16[3,1536,128]{2,1,0:T(8,128)(2,1)S(1)}, bf16[3,1536,384]{2,1,0:T(8,128)(2,1)}, s32[]{:T(128)}, s32[]{:T(128)}, /*index=5*/s32[]{:T(128)}) while((s32[]{:T(128)}, bf16[3,1536,128]{2,1,0:T(8,128)(2,1)S(1)}, bf16[3,1536,384]{2,1,0:T(8,128)(2,1)}, s32[]{:T(128)}, s32[]{:T(128)}, /*index=5*/s32[]{:T(128)}) %tuple.77), condition=%wide.region_7.8_spmd, body=%wide.region_2.7_spmd.sunk | while | flops 408222720 | bytes 16001234 | solution.py:76
  273.4 1.4 dynamic-slice_bitcast_fusion.2
  275.0 6.1 %while.33 = (s32[]{:T(128)}, bf16[3,512,128]{2,1,0:T(8,128)(2,1)S(1)}, bf16[3,512,128]{2,1,0:T(8,128)(2,1)S(1)}, bf16[1536,128]{1,0:T(8,128)(2,1)S(1)}, bf16[1536,128]{1,0:T(8,128)(2,1)S(1)}, /*index=5*/s32[]{:T(128)}) while((s32[]{:T(128)}, bf16[3,512,128]{2,1,0:T(8,128)(2,1)S(1)}, bf16[3,512,128]{2,1,0:T(8,128)(2,1)S(1)}, ...), condition=%wide.region_6.6_spmd, body=%wide.region_3.5_spmd.sunk | while | flops 408222720 | bytes 10496077 | solution.py:71
  275.0 0.7 fusion.64
  275.7 0.6 fusion.65
  276.3 0.8 fusion.66
  277.1 0.7 fusion.64
  277.7 0.6 fusion.65
  278.3 0.8 fusion.66
  279.1 0.7 fusion.64
  280.3 0.8 fusion.66
  281.2 1.4 dynamic-slice_bitcast_fusion.2
  282.8 6.1 %while.33 = (s32[]{:T(128)}, bf16[3,512,128]{2,1,0:T(8,128)(2,1)S(1)}, bf16[3,512,128]{2,1,0:T(8,128)(2,1)S(1)}, bf16[1536,128]{1,0:T(8,128)(2,1)S(1)}, bf16[1536,128]{1,0:T(8,128)(2,1)S(1)}, /*index=5*/s32[]{:T(128)}) while((s32[]{:T(128)}, bf16[3,512,128]{2,1,0:T(8,128)(2,1)S(1)}, bf16[3,512,128]{2,1,0:T(8,128)(2,1)S(1)}, ...), condition=%wide.region_6.6_spmd, body=%wide.region_3.5_spmd.sunk | while | flops 408222720 | bytes 10496077 | solution.py:71
  282.8 0.7 fusion.64
  283.5 0.6 fusion.65
  284.0 0.8 fusion.66
  284.8 0.7 fusion.64
  286.1 0.8 fusion.66
  286.9 0.7 fusion.64
  288.1 0.8 fusion.66
  289.0 1.4 dynamic-slice_bitcast_fusion.2
  290.6 6.1 %while.33 = (s32[]{:T(128)}, bf16[3,512,128]{2,1,0:T(8,128)(2,1)S(1)}, bf16[3,512,128]{2,1,0:T(8,128)(2,1)S(1)}, bf16[1536,128]{1,0:T(8,128)(2,1)S(1)}, bf16[1536,128]{1,0:T(8,128)(2,1)S(1)}, /*index=5*/s32[]{:T(128)}) while((s32[]{:T(128)}, bf16[3,512,128]{2,1,0:T(8,128)(2,1)S(1)}, bf16[3,512,128]{2,1,0:T(8,128)(2,1)S(1)}, ...), condition=%wide.region_6.6_spmd, body=%wide.region_3.5_spmd.sunk | while | flops 408222720 | bytes 10496077 | solution.py:71
  290.6 0.7 fusion.64
  291.8 0.8 fusion.66
  292.6 0.7 fusion.64
  293.8 0.8 fusion.66
  294.6 0.7 fusion.64
  295.3 0.6 fusion.65
  295.9 0.8 fusion.66
  296.7 8.2 %copy.32 = bf16[3,1536,128]{2,0,1:T(4,128)(2,1)} copy(bf16[3,1536,128]{2,1,0:T(8,128)(2,1)S(1)} %get-tuple-element.69) | data formatting | bytes 2359296 | tf_op jit(solution)/shard_map/while | solution.py:76
  304.9 7.0 %all-to-all-start.2 = ((bf16[1,3,1536,128]{3,1,0,2:T(4,128)(2,1)}), bf16[1,3,1536,128]{3,1,0,2:T(4,128)(2,1)}, u32[]{:S(2)}, u32[]{:S(2)}) async-start(bf16[1,3,1536,128]{3,1,0,2:T(4,128)(2,1)} %bitcast.71), calls=%async_computation.2 | async-start | bytes 3145728 | tf_op jit(solution)/shard_map/all_to_all | solution.py:131
  312.1 22.2 %all-to-all-done.2 = bf16[1,3,1536,128]{3,1,0,2:T(4,128)(2,1)} async-done(((bf16[1,3,1536,128]{3,1,0,2:T(4,128)(2,1)}), bf16[1,3,1536,128]{3,1,0,2:T(4,128)(2,1)}, u32[]{:S(2)}, u32[]{:S(2)}) %all-to-all-start.2) | async-done | bytes 1179680 | tf_op jit(solution)/shard_map/all_to_all | solution.py:131
  334.3 1.6 copy.20
  336.0 4.4 fusion.50
  342.0 22.7 %all_gather.7 = f32[8,48,64]{2,1,0:T(8,128)S(1)} all-gather(f32[1,48,64]{2,1,0:T(8,128)S(1)} %slice.39), channel_id=1, replica_groups=mesh['tm'=8,'seq'=32] {'tm'}, dimensions={0}, use_global_device_ids=true | all-gather | bytes 110592 | tf_op jit(solution)/shard_map/all_gather | solution.py:16
  364.8 0.7 multiply_reduce_fusion.2
  365.5 70.3 %psum.7 = f32[8]{0:T(128)S(1)} all-reduce(f32[8]{0:T(128)S(1)} %get-tuple-element.95), channel_id=1, replica_groups=mesh['tm'=8,'seq'=32] {'seq'}, use_global_device_ids=true, to_apply=%region_14.15 | all-reduce | flops 8 | bytes 64 | tf_op jit(solution)/shard_map/psum | solution.py:154
  (76 shorter events, 8.1 us)
Async XLA Ops:
  7.2 21.1 %copy-start = (bf16[256,4608]{1,0:T(8,128)(2,1)S(1)}, bf16[256,4608]{1,0:T(8,128)(2,1)}, u32[]{:S(2)}) copy-start(bf16[256,4608]{1,0:T(8,128)(2,1)} %param.20) | copy-start | bytes 7077892
  15.6 8.8 %copy-start.6 = (f32[8,48,64]{2,1,0:T(8,128)S(1)}, f32[8,48,64]{2,1,0:T(8,128)}, u32[]{:S(2)}) copy-start(f32[8,48,64]{2,1,0:T(8,128)} %param.15) | copy-start | bytes 294916
  15.6 12.5 %copy-start.14 = (s32[8]{0:T(128)S(1)}, s32[8]{0:T(128)}, u32[]{:S(2)}) copy-start(s32[8]{0:T(128)} %param.17) | copy-start | bytes 100
  15.6 179.5 %all-to-all-start = ((bf16[32,48,12,384]{3,1,2,0:T(8,128)(2,1)}), bf16[32,48,12,384]{3,1,2,0:T(8,128)(2,1)}, u32[]{:S(2)}, u32[]{:S(2)}) async-start(bf16[32,48,12,384]{3,1,2,0:T(8,128)(2,1)} %stack.2), calls=%async_computation | async-start | bytes 28311552 | tf_op jit(solution)/shard_map/all_to_all | solution.py:123
  24.4 5.0 %copy-start.12 = (f32[48,64]{1,0:T(8,128)S(1)}, f32[48,64]{1,0:T(8,128)}, u32[]{:S(2)}) copy-start(f32[48,64]{1,0:T(8,128)} %param.16) | copy-start | bytes 36868
  24.4 5.6 %copy-start.11 = (bf16[64,1536]{1,0:T(8,128)(2,1)S(1)}, bf16[64,1536]{1,0:T(8,128)(2,1)}, u32[]{:S(2)}) copy-start(bf16[64,1536]{1,0:T(8,128)(2,1)} %param.19) | copy-start | bytes 589828
  24.4 4.9 %collective-permute-start = (f32[48,64]{1,0:T(8,128)S(1)}, f32[48,64]{1,0:T(8,128)S(1)}, u32[]{:S(2)}, u32[]{:S(2)}) collective-permute-start(f32[48,64]{1,0:T(8,128)S(1)} %slice_bitcast_fusion), channel_id=1, source_target_pairs={{0,32},{32,64},{64,96},{96,128},{128,160},{160,192},{192,224},{1,3... | collective-permute-start | bytes 36872 | tf_op jit(solution)/shard_map/ppermute | solution.py:11
  29.3 1.6 copy-start.4
  29.4 0.6 copy-start.8
  30.5 171.4 %copy-start.2 = (f32[8,48,1536]{2,1,0:T(8,128)}, f32[8,48,1536]{2,1,0:T(8,128)S(1)}, u32[]{:S(2)}) copy-start(f32[8,48,1536]{2,1,0:T(8,128)S(1)} %get-tuple-element.110) | copy-start | bytes 7077892
  209.4 59.9 %all-to-all-start.1 = ((bf16[32,3,48,384]{3,2,1,0:T(8,128)(2,1)}), bf16[32,3,48,384]{3,2,1,0:T(8,128)(2,1)}, u32[]{:S(2)}, u32[]{:S(2)}) async-start(bf16[32,3,48,384]{3,2,1,0:T(8,128)(2,1)} %bitcast.93), calls=%async_computation.1 | async-start | bytes 7077888 | tf_op jit(solution)/shard_map/all_to_all | solution.py:130
  223.7 112.3 %all-gather.2.cloned.1.call-start = ((), (), s32[]{:S(2)}) async-start(), calls=%async_computation.3 | async-start | bytes 4866048 | tf_op jit(solution)/shard_map/all_gather | solution.py:139
  296.7 15.2 %copy-start.15 = (s32[8]{0:T(128)S(1)}, s32[8]{0:T(128)}, u32[]{:S(2)}) copy-start(s32[8]{0:T(128)} %param.17) | copy-start | bytes 100
  296.7 15.2 %copy-start.16 = (s32[8]{0:T(128)S(1)}, s32[8]{0:T(128)}, u32[]{:S(2)}) copy-start(s32[8]{0:T(128)} %param.18) | copy-start | bytes 100
  304.9 29.4 %all-to-all-start.2 = ((bf16[1,3,1536,128]{3,1,0,2:T(4,128)(2,1)}), bf16[1,3,1536,128]{3,1,0,2:T(4,128)(2,1)}, u32[]{:S(2)}, u32[]{:S(2)}) async-start(bf16[1,3,1536,128]{3,1,0,2:T(4,128)(2,1)} %bitcast.71), calls=%async_computation.2 | async-start | bytes 3145728 | tf_op jit(solution)/shard_map/all_to_all | solution.py:131
  312.1 23.9 %copy-start.3 = (f32[8,48,1536]{2,1,0:T(8,128)S(1)}, f32[8,48,1536]{2,1,0:T(8,128)}, u32[]{:S(2)}) copy-start(f32[8,48,1536]{2,1,0:T(8,128)} %copy-done.2) | copy-start | bytes 7077892
  340.4 0.9 copy-start.10
  340.5 1.4 copy-start.5
  340.5 1.4 copy-start.9
  340.9 23.9 %copy-start.13 = (f32[48,64]{1,0:T(8,128)S(1)}, f32[48,64]{1,0:T(8,128)}, u32[]{:S(2)}) copy-start(f32[48,64]{1,0:T(8,128)} %param.16) | copy-start | bytes 36868
  340.9 23.9 %copy-start.7 = (f32[8,48,64]{2,1,0:T(8,128)S(1)}, f32[8,48,64]{2,1,0:T(8,128)}, u32[]{:S(2)}) copy-start(f32[8,48,64]{2,1,0:T(8,128)} %param.15) | copy-start | bytes 294916
  340.9 95.5 %copy-start.1 = (bf16[256,4608]{1,0:T(8,128)(2,1)S(1)}, bf16[256,4608]{1,0:T(8,128)(2,1)}, u32[]{:S(2)}) copy-start(bf16[256,4608]{1,0:T(8,128)(2,1)} %param.20) | copy-start | bytes 7077892
Sparse Core Ops, SparseCore 0:
  227.0 70.1 all-gather.1
